TPU v7x, 32 devices: a whole 2x2x4 slice. The times are simulated.
32 devices in a mesh: groups: 2 (over x), pts: 16 (over z, y, core).
Axes of the slice: x: 2, y: 2, z: 4, core: 2. Of those that a mesh axis runs over, the one named last changes fastest.
Arguments:
- points: bfloat16 [8192, 512], P(('groups', 'pts')), parts along dimension 0, may hold values from -6 to 6
- labels: int32 [8192], P(('groups', 'pts')), parts along dimension 0, may hold values from 0 to 15
- centres: bfloat16 [32768, 512], P(('groups', 'pts')), parts along dimension 0, may hold values from -6 to 6
- tri_inverse: bfloat16 [32768, 16384], P(('groups', 'pts')), parts along dimension 0, as said below
- beta: bfloat16 [32768, 16], P(('groups', 'pts')), parts along dimension 0, may hold values from -0.01171875 to 0.01171875
- bias: float32 [32], P('groups'), parts along dimension 0, may hold values from -3.2 to -2.2
Outputs:
- gradient: float32 [32768, 16], P(('groups', 'pts')), parts along dimension 0
- logits: float32 [8192, 16], P(('groups', 'pts')), parts along dimension 0
There are 2 independent parts, one for each index of `groups`. A program takes and returns all parts, laid end to end along the dimension named above; each array names one. Nothing has to cross between parts.
Inputs may be any that keep to these rules, and one draw needn't show every extreme that they name: `tri_inverse`: upper triangular: entries below the diagonal are zero; the diagonal lies between 0.6 and 1.4.
All inputs are finite; a program needn't handle non-finite values.
Results may differ from a plain program's by a relative error of at most 0.0039.
Values may be sent and summed in bfloat16 or wider, within the bound.
A program may use at most 128 MiB of HBM per device.

v0:
```python
import math
import jax
import jax.numpy as jnp
from jax import lax
from jax.sharding import PartitionSpec as P


def cube_kernel(point_block, centre_block):
    inner = lax.dot_general(
        point_block, centre_block, (((1,), (1,)), ((), ())), preferred_element_type=jnp.float32
    )
    factor = 1.0 / math.sqrt(point_block.shape[1])
    return ((inner * factor + 1.0) ** 3).astype(jnp.bfloat16)


def on_device(points, labels, centres, tri_inverse, beta, bias):
    local_points = points.shape[0]
    local_centres = centres.shape[0]
    class_count = beta.shape[1]
    packing = 128 // class_count
    dense_centres = local_centres // packing
    total_points = local_points * lax.axis_size("pts")
    beta_dense = beta.reshape(dense_centres, 128)
    beta_part = lax.all_gather(beta_dense, "pts", axis=0, tiled=True)
    narrow = beta_part.reshape(beta_part.shape[0] * packing, class_count)
    columns = tri_inverse
    alpha_sum = jnp.dot(columns, narrow, preferred_element_type=jnp.float32)
    alpha_local = alpha_sum.astype(jnp.bfloat16)
    alpha_dense = alpha_local.reshape(dense_centres, 128)
    classes_row = jnp.arange(class_count, dtype=jnp.int32)
    onehot = (labels[:, None] == classes_row[None, :]).astype(jnp.float32)
    parts_in = (
        lax.all_gather(centres, "pts", axis=0, tiled=True),
        lax.all_gather(alpha_dense, "pts", axis=0, tiled=True),
    )
    kernel_tile = cube_kernel(points, parts_in[0])
    narrow = parts_in[1].reshape(parts_in[1].shape[0] * packing, class_count)
    logit_sum = jnp.dot(kernel_tile, narrow, preferred_element_type=jnp.float32)
    logits = logit_sum + bias[None, :]
    resid = (jax.nn.sigmoid(logits) - onehot).astype(jnp.bfloat16)
    resid_dense = resid.reshape(local_points // packing, 128)
    parts_in = (
        lax.all_gather(points, "pts", axis=0, tiled=True),
        lax.all_gather(resid_dense, "pts", axis=0, tiled=True),
    )
    kernel_tile = cube_kernel(parts_in[0], centres)
    narrow = parts_in[1].reshape(parts_in[1].shape[0] * packing, class_count)
    grad_sum = lax.dot_general(
        kernel_tile, narrow, (((0,), (0,)), ((), ())), preferred_element_type=jnp.float32
    )
    grad_dense = grad_sum.reshape(dense_centres, 128)
    grad_kernel = (
        grad_dense.reshape(local_centres, class_count) * (1.0 / math.sqrt(total_points))
    ).astype(jnp.bfloat16)
    columns = tri_inverse
    term = lax.dot_general(
        columns, grad_kernel, (((0,), (0,)), ((), ())), preferred_element_type=jnp.float32
    )
    gradient_dense = lax.psum_scatter(
        term.reshape(lax.axis_size("pts") * dense_centres, 128),
        "pts",
        scatter_dimension=0,
        tiled=True,
    )
    return (gradient_dense.reshape(local_centres, class_count), logits)


def solution(mesh):
    return jax.shard_map(
        on_device,
        mesh=mesh,
        in_specs=(
            P(("groups", "pts"), None),
            P(("groups", "pts")),
            P(("groups", "pts"), None),
            P(("groups", "pts"), None),
            P(("groups", "pts"), None),
            P("groups"),
        ),
        out_specs=(P(("groups", "pts"), None), P(("groups", "pts"), None)),
        check_vma=False,
    )
```

profile of v0, /device:TPU:0, one launch (start us, length us, event | category | flops | bytes accessed | tf_op | source)
XLA Modules:
  0.0 295.3 jit_solution(16298011855423108095)
XLA Ops:
  7.2 0.0 all-gather.5.cloned.1.call-start
  7.2 0.7 all-gather.5.cloned.1.call-update
  7.9 0.0 all-gather.3.cloned.1.call-start
  7.9 0.7 all-gather.3.cloned.1.call-update
  8.6 0.0 reduce-scatter.2.cloned.1.call-start
  8.7 0.9 copy.8
  9.6 0.2 reshape.30
  9.8 26.4 %all_gather.17 = bf16[2048,128]{1,0:T(8,128)(2,1)S(1)} all-gather(bf16[128,128]{1,0:T(8,128)(2,1)S(1)} %reshape.30), channel_id=1, replica_groups=mesh['groups'=2,'pts'=16] {'pts'}, dimensions={0}, use_global_device_ids=true | all-gather | bytes 557056 | tf_op jit(solution)/shard_map/all_gather | solution.py:24
  36.3 4.0 %reshape.31 = bf16[16384,16]{1,0:T(8,128)(2,1)} reshape(bf16[2048,128]{1,0:T(8,128)(2,1)S(1)} %all_gather.17) | data formatting | bytes 1048576 | tf_op jit(solution)/shard_map/reshape | solution.py:25
  40.3 15.4 %convolution_convert_fusion = bf16[1024,16]{0,1:T(8,128)(2,1)S(1)} fusion(bf16[1024,16384]{1,0:T(8,128)(2,1)} %param.9, bf16[16384,16]{1,0:T(8,128)(2,1)} %reshape.31), kind=kOutput, calls=%fused_computation.11 | convolution fusion | flops 536887296 | bytes 34111488 | tf_op jit(solution)/shard_map/dot_general | solution.py:27
  55.7 0.2 copy.9
  55.9 0.2 reshape.32
  56.0 20.5 %all_gather.18 = bf16[2048,128]{1,0:T(8,128)(2,1)S(1)} all-gather(bf16[128,128]{1,0:T(8,128)(2,1)S(1)} %reshape.32), channel_id=1, replica_groups=mesh['groups'=2,'pts'=16] {'pts'}, dimensions={0}, use_global_device_ids=true | all-gather | bytes 557056 | tf_op jit(solution)/shard_map/all_gather | solution.py:34
  76.5 4.0 %reshape.33 = bf16[16384,16]{1,0:T(8,128)(2,1)} reshape(bf16[2048,128]{1,0:T(8,128)(2,1)S(1)} %all_gather.18) | data formatting | bytes 1048576 | tf_op jit(solution)/shard_map/reshape | solution.py:37
  80.5 61.5 %all-gather.5.cloned.1.call-done = bf16[16384,512]{1,0:T(8,128)(2,1)} async-done(((bf16[1024,512]{1,0:T(8,128)(2,1)}), bf16[16384,512]{1,0:T(8,128)(2,1)}) %all-gather.5.cloned.1.call-update) | async-done | bytes 16777232 | tf_op jit(solution)/shard_map/all_gather | solution.py:33
  142.0 0.0 copy-done.1
  142.0 0.0 copy-done.2
  142.0 0.0 copy-done.3
  142.0 11.7 %subtract_convert_fusion = (bf16[256,16]{0,1:T(8,128)(2,1)S(1)}, f32[256,16]{0,1:T(8,128)}) fusion(s32[256]{0:T(256)S(1)} %copy-done.2, f32[16]{0:T(128)S(1)} %copy-done.3, bf16[16384,16]{1,0:T(8,128)(2,1)} %reshape.33, bf16[256,512]{1,0:T(8,128)(2,1)S(1)} %copy-done.1, bf16[16384,512]{1,0:T(8,128)(2,1)} %all-gather.5.cloned.1.call-done), kind=kOutput, calls=%fused_computation.13 | convolution fusion | flops 4450189312 | bytes 17589312 | tf_op jit(solution)/shard_map/dot_general | solution.py:38
  153.7 0.1 copy.10
  153.8 0.1 reshape.34
  153.9 18.6 %all_gather.19 = bf16[512,128]{1,0:T(8,128)(2,1)S(1)} all-gather(bf16[32,128]{1,0:T(8,128)(2,1)S(1)} %reshape.34), channel_id=1, replica_groups=mesh['groups'=2,'pts'=16] {'pts'}, dimensions={0}, use_global_device_ids=true | all-gather | bytes 139264 | tf_op jit(solution)/shard_map/all_gather | solution.py:44
  172.6 0.7 reshape.35
  173.2 20.2 %all-gather.3.cloned.1.call-done = bf16[4096,512]{1,0:T(8,128)(2,1)} async-done(((bf16[256,512]{1,0:T(8,128)(2,1)}), bf16[4096,512]{1,0:T(8,128)(2,1)}) %all-gather.3.cloned.1.call-update) | async-done | bytes 4194320 | tf_op jit(solution)/shard_map/all_gather | solution.py:43
  193.5 12.9 %fusion.10 = bf16[1024,16]{1,0:T(8,128)(2,1)S(1)} fusion(bf16[4096,16]{1,0:T(8,128)(2,1)S(1)} %reshape.35, bf16[4096,512]{1,0:T(8,128)(2,1)} %all-gather.3.cloned.1.call-done, bf16[1024,512]{1,0:T(8,128)(2,1)S(1)} %copy-done), kind=kOutput, calls=%fused_computation.10 | convolution fusion | flops 4450189312 | bytes 5406720 | tf_op jit(solution)/shard_map/dot_general | solution.py:48
  206.4 13.1 %convolution_bitcast_fusion = f32[16384,16]{0,1:T(8,128)S(1)} fusion(bf16[1024,16]{1,0:T(8,128)(2,1)S(1)} %fusion.10, bf16[1024,16384]{1,0:T(8,128)(2,1)} %param.9), kind=kOutput, calls=%fused_computation.5 | convolution fusion | flops 536870912 | bytes 34635776 | tf_op jit(solution)/shard_map/dot_general | solution.py:56
  219.4 4.6 %copy.11 = f32[16384,16]{1,0:T(8,128)} copy(f32[16384,16]{0,1:T(8,128)S(1)} %convolution_bitcast_fusion) | data formatting | bytes 2097152 | tf_op jit(solution)/shard_map/dot_general | solution.py:56
  224.0 6.5 %reshape.36 = f32[2048,128]{1,0:T(8,128)} reshape(f32[16384,16]{1,0:T(8,128)} %copy.11) | data formatting | bytes 2097152 | tf_op jit(solution)/shard_map/reshape | solution.py:60
  230.5 0.0 reduce-scatter.2.cloned.1.call-update
  230.5 56.4 %reduce-scatter.2.cloned.1.call-done = f32[128,128]{1,0:T(8,128)} async-done(((f32[2048,128]{1,0:T(8,128)}), f32[128,128]{1,0:T(8,128)}) %reduce-scatter.2.cloned.1.call-update) | async-done | bytes 65552 | tf_op jit(solution)/shard_map/reduce_scatter | solution.py:59
  286.9 1.0 reshape.37
  288.0 0.8 copy.12
  (5 shorter events, 0.0 us)
Async XLA Ops:
  7.2 134.8 %all-gather.5.cloned.1.call-start = ((), (), s32[]{:S(2)}) async-start(), calls=%async_computation.2 | async-start | bytes 17825792 | tf_op jit(solution)/shard_map/all_gather | solution.py:33
  7.9 185.6 %all-gather.3.cloned.1.call-start = ((), (), s32[]{:S(2)}) async-start(), calls=%async_computation.1 | async-start | bytes 4456448 | tf_op jit(solution)/shard_map/all_gather | solution.py:43
  8.6 278.3 %reduce-scatter.2.cloned.1.call-start = ((), (), s32[]{:S(2)}) async-start(), calls=%async_computation.3 | async-start | bytes 1114112 | tf_op jit(solution)/shard_map/reduce_scatter | solution.py:59
  40.3 101.7 %copy-start.1 = (bf16[256,512]{1,0:T(8,128)(2,1)S(1)}, bf16[256,512]{1,0:T(8,128)(2,1)}, u32[]{:S(2)}) copy-start(bf16[256,512]{1,0:T(8,128)(2,1)} %param.6) | copy-start | bytes 786436
  40.3 101.7 %copy-start.2 = (s32[256]{0:T(256)S(1)}, s32[256]{0:T(256)}, u32[]{:S(2)}) copy-start(s32[256]{0:T(256)} %param.7) | copy-start | bytes 3076
  40.3 101.7 %copy-start.3 = (f32[16]{0:T(128)S(1)}, f32[16]{0:T(128)}, u32[]{:S(2)}) copy-start(f32[16]{0:T(128)} %param.11) | copy-start | bytes 196
  80.5 112.9 %copy-start = (bf16[1024,512]{1,0:T(8,128)(2,1)S(1)}, bf16[1024,512]{1,0:T(8,128)(2,1)}, u32[]{:S(2)}) copy-start(bf16[1024,512]{1,0:T(8,128)(2,1)} %param.8) | copy-start | bytes 3145732
Sparse Core Ops, SparseCore 0:
  10.1 131.8 all-gather.4
  144.2 49.2 all-gather.2
  230.6 56.2 reduce-scatter.1
where the time goes:
time: 296 us; the launch traced here: 295 us
  waiting for transfers between devices  140 us (47%)
  blocking collectives  65.5 us (22%)
  matrix products  53.1 us (18%)
  local copies, waits for them, and re-layouts  23.3 us (8%)
  between operations  13.8 us (5%)
    all_gather x1, waiting for transfers between devices, on_device(): lax.all_gather(centres, 'pts', axis=0, tiled=True)  61.5 us
    reduce_scatter x1, waiting for transfers between devices, on_device(): lax.psum_scatter(term.reshape(lax.axis_size('pts') * dense_centres, 128),...  56.4 us
    all_gather x1, blocking collectives, on_device(): beta_part = lax.all_gather(beta_dense, 'pts', axis=0, tiled=True)  26.4 us
    all_gather x1, blocking collectives, on_device(): lax.all_gather(alpha_dense, 'pts', axis=0, tiled=True)  20.5 us
    all_gather x1, waiting for transfers between devices, on_device(): lax.all_gather(points, 'pts', axis=0, tiled=True)  20.2 us
    all_gather x1, blocking collectives, on_device(): lax.all_gather(resid_dense, 'pts', axis=0, tiled=True)  18.6 us
    dot_general x1, matrix products, on_device(): alpha_sum = jnp.dot(columns, narrow, preferred_element_type=jnp.float32)  15.4 us
    dot_general x1, matrix products, on_device(): lax.dot_general(columns, grad_kernel, (((0,), (0,)), ((), ())), preferred...  13.1 us
  transfers between devices with their start and end apart: 3, of which 3 were waited for; matrix products, arithmetic and copies ran while one was open for 13% of the time, Pallas kernels for 0%

commit v1 on v0

--- a/solution.py
+++ b/solution.py
@@ -3,6 +3,19 @@
 import jax.numpy as jnp
 from jax import lax
 from jax.sharding import PartitionSpec as P
+
+
+def ring_gather(x, axis, dim):
+    ways = lax.axis_size(axis)
+    up = [(d, (d + 1) % ways) for d in range(ways)]
+    down = [(d, (d - 1) % ways) for d in range(ways)]
+    earlier, later = ([x], [x])
+    for _ in range(ways // 2):
+        earlier.append(lax.ppermute(earlier[-1], axis, up))
+    for _ in range((ways - 1) // 2):
+        later.append(lax.ppermute(later[-1], axis, down))
+    line = jnp.concatenate([*earlier[::-1], *later[1:]], axis=dim)
+    return jnp.roll(line, (lax.axis_index(axis) - ways // 2) * x.shape[dim], axis=dim)
 
 
 def cube_kernel(point_block, centre_block):
@@ -40,7 +53,7 @@
     resid = (jax.nn.sigmoid(logits) - onehot).astype(jnp.bfloat16)
     resid_dense = resid.reshape(local_points // packing, 128)
     parts_in = (
-        lax.all_gather(points, "pts", axis=0, tiled=True),
+        ring_gather(points, "pts", 0),
         lax.all_gather(resid_dense, "pts", axis=0, tiled=True),
     )
     kernel_tile = cube_kernel(parts_in[0], centres)

time: 296 us -> 328 us (1.11)
  waiting for transfers between devices: 140 us -> 103 us
  local copies, waits for them, and re-layouts: 23.3 us -> 53.1 us
  starting transfers between devices: 0.11 us -> 27.6 us
  blocking collectives: 65.5 us -> 76.6 us
    all_gather x1, waiting for transfers between devices: 61.5 us -> 0.01 us  [on_device(): lax.all_gather(centres, 'pts', axis=0, tiled=True)]
    ppermute x0 -> x15, waiting for transfers between devices: none -> 47.2 us  [the longest x8 30.5 us: ring_gather(): earlier.append(lax.ppermute(earlier[-1], axis, up))]
    unnamed x10 -> x45, local copies, waits for them, and re-layouts: 1.74 us -> 30.7 us
    ppermute x0 -> x15, starting transfers between devices: none -> 27.5 us  [the longest x7 27 us: ring_gather(): later.append(lax.ppermute(later[-1], axis, down))]
    all_gather x1 -> x0, waiting for transfers between devices: 20.2 us -> none  [on_device(): lax.all_gather(points, 'pts', axis=0, tiled=True)]
    all_gather x1, blocking collectives: 26.4 us -> 32.9 us  [on_device(): beta_part = lax.all_gather(beta_dense, 'pts', axis=0, tiled=True)]
  transfers between devices with their start and end apart: 3 -> 17, of which waited for: 3 -> 10; matrix products, arithmetic and copies ran while one was open for 13% -> 17% of each run, Pallas kernels for 0% -> 0%
where the time goes in v1:
time: 328 us
  waiting for transfers between devices  103 us (31%)
  blocking collectives  76.6 us (23%)
  local copies, waits for them, and re-layouts  53.1 us (16%)
  matrix products  53 us (16%)
  starting transfers between devices  27.6 us (8%)
  between operations  14.2 us (4%)
    reduce_scatter x1, waiting for transfers between devices, on_device(): lax.psum_scatter(term.reshape(lax.axis_size('pts') * dense_centres, 128),...  55.2 us
    all_gather x1, blocking collectives, on_device(): beta_part = lax.all_gather(beta_dense, 'pts', axis=0, tiled=True)  32.9 us
    unnamed x45, local copies, waits for them, and re-layouts  30.7 us
    ppermute x8, waiting for transfers between devices, ring_gather(): earlier.append(lax.ppermute(earlier[-1], axis, up))  30.5 us
    ppermute x7, starting transfers between devices, ring_gather(): later.append(lax.ppermute(later[-1], axis, down))  27 us
    all_gather x1, blocking collectives, on_device(): lax.all_gather(alpha_dense, 'pts', axis=0, tiled=True)  23.3 us
    all_gather x1, blocking collectives, on_device(): lax.all_gather(resid_dense, 'pts', axis=0, tiled=True)  20.3 us
    ppermute x7, waiting for transfers between devices, ring_gather(): later.append(lax.ppermute(later[-1], axis, down))  16.7 us
  transfers between devices with their start and end apart: 17, of which 10 were waited for; matrix products, arithmetic and copies ran while one was open for 17% of the time, Pallas kernels for 0%

profile of v1, /device:TPU:0, one launch (start us, length us, event | category | flops | bytes accessed | tf_op | source)
XLA Modules:
  0.0 327.6 jit_solution(6182492206873567492)
XLA Ops:
  8.5 9.2 %collective-permute-done = bf16[256,512]{1,0:T(8,128)(2,1)S(1)} collective-permute-done((bf16[256,512]{1,0:T(8,128)(2,1)}, bf16[256,512]{1,0:T(8,128)(2,1)S(1)}, u32[]{:S(2)}, u32[]{:S(2)}) %collective-permute-start) | collective-permute-done | bytes 262176 | tf_op jit(solution)/shard_map/ppermute | solution.py:14
  17.7 4.4 %collective-permute-start.8 = (bf16[256,512]{1,0:T(8,128)(2,1)}, bf16[256,512]{1,0:T(8,128)(2,1)S(1)}, u32[]{:S(2)}, u32[]{:S(2)}) collective-permute-start(bf16[256,512]{1,0:T(8,128)(2,1)} %param.6), channel_id=1, source_target_pairs={{0,15},{1,0},{2,1},{3,2},{4,3},{5,4},{6,5},{7,6},{8,7},{9,8},{10,9... | collective-permute-start | bytes 786440 | tf_op jit(solution)/shard_map/ppermute | solution.py:16
  22.2 4.1 %collective-permute-done.1 = bf16[256,512]{1,0:T(8,128)(2,1)S(1)} collective-permute-done((bf16[256,512]{1,0:T(8,128)(2,1)S(1)}, bf16[256,512]{1,0:T(8,128)(2,1)S(1)}, u32[]{:S(2)}, u32[]{:S(2)}) %collective-permute-start.1) | collective-permute-done | bytes 262176 | tf_op jit(solution)/shard_map/ppermute | solution.py:14
  26.3 5.6 %collective-permute-done.8 = bf16[256,512]{1,0:T(8,128)(2,1)S(1)} collective-permute-done((bf16[256,512]{1,0:T(8,128)(2,1)}, bf16[256,512]{1,0:T(8,128)(2,1)S(1)}, u32[]{:S(2)}, u32[]{:S(2)}) %collective-permute-start.8) | collective-permute-done | bytes 262176 | tf_op jit(solution)/shard_map/ppermute | solution.py:16
  32.0 4.5 %collective-permute-start.9 = (bf16[256,512]{1,0:T(8,128)(2,1)S(1)}, bf16[256,512]{1,0:T(8,128)(2,1)S(1)}, u32[]{:S(2)}, u32[]{:S(2)}) collective-permute-start(bf16[256,512]{1,0:T(8,128)(2,1)S(1)} %collective-permute-done.8), channel_id=1, source_target_pairs={{0,15},{1,0},{2,1},{3,2},{4,3},{5,4},{6,5},{7,6},{8,7},{9,8},{10,9... | collective-permute-start | bytes 786440 | tf_op jit(solution)/shard_map/ppermute | solution.py:16
  36.5 4.1 %collective-permute-done.2 = bf16[256,512]{1,0:T(8,128)(2,1)S(1)} collective-permute-done((bf16[256,512]{1,0:T(8,128)(2,1)S(1)}, bf16[256,512]{1,0:T(8,128)(2,1)S(1)}, u32[]{:S(2)}, u32[]{:S(2)}) %collective-permute-start.2) | collective-permute-done | bytes 262176 | tf_op jit(solution)/shard_map/ppermute | solution.py:14
  40.6 5.5 %collective-permute-done.9 = bf16[256,512]{1,0:T(8,128)(2,1)S(1)} collective-permute-done((bf16[256,512]{1,0:T(8,128)(2,1)S(1)}, bf16[256,512]{1,0:T(8,128)(2,1)S(1)}, u32[]{:S(2)}, u32[]{:S(2)}) %collective-permute-start.9) | collective-permute-done | bytes 262176 | tf_op jit(solution)/shard_map/ppermute | solution.py:16
  46.1 4.6 %collective-permute-start.10 = (bf16[256,512]{1,0:T(8,128)(2,1)S(1)}, bf16[256,512]{1,0:T(8,128)(2,1)S(1)}, u32[]{:S(2)}, u32[]{:S(2)}) collective-permute-start(bf16[256,512]{1,0:T(8,128)(2,1)S(1)} %collective-permute-done.9), channel_id=1, source_target_pairs={{0,15},{1,0},{2,1},{3,2},{4,3},{5,4},{6,5},{7,6},{8,7},{9,8},{10,9... | collective-permute-start | bytes 786440 | tf_op jit(solution)/shard_map/ppermute | solution.py:16
  50.7 4.1 %collective-permute-done.3 = bf16[256,512]{1,0:T(8,128)(2,1)S(1)} collective-permute-done((bf16[256,512]{1,0:T(8,128)(2,1)S(1)}, bf16[256,512]{1,0:T(8,128)(2,1)S(1)}, u32[]{:S(2)}, u32[]{:S(2)}) %collective-permute-start.3) | collective-permute-done | bytes 262176 | tf_op jit(solution)/shard_map/ppermute | solution.py:14
  54.8 5.5 %collective-permute-done.10 = bf16[256,512]{1,0:T(8,128)(2,1)S(1)} collective-permute-done((bf16[256,512]{1,0:T(8,128)(2,1)S(1)}, bf16[256,512]{1,0:T(8,128)(2,1)S(1)}, u32[]{:S(2)}, u32[]{:S(2)}) %collective-permute-start.10) | collective-permute-done | bytes 262176 | tf_op jit(solution)/shard_map/ppermute | solution.py:16
  60.4 4.6 %collective-permute-start.11 = (bf16[256,512]{1,0:T(8,128)(2,1)S(1)}, bf16[256,512]{1,0:T(8,128)(2,1)S(1)}, u32[]{:S(2)}, u32[]{:S(2)}) collective-permute-start(bf16[256,512]{1,0:T(8,128)(2,1)S(1)} %collective-permute-done.10), channel_id=1, source_target_pairs={{0,15},{1,0},{2,1},{3,2},{4,3},{5,4},{6,5},{7,6},{8,7},{9,8},{10,9... | collective-permute-start | bytes 786440 | tf_op jit(solution)/shard_map/ppermute | solution.py:16
  65.0 4.1 %collective-permute-done.4 = bf16[256,512]{1,0:T(8,128)(2,1)S(1)} collective-permute-done((bf16[256,512]{1,0:T(8,128)(2,1)S(1)}, bf16[256,512]{1,0:T(8,128)(2,1)S(1)}, u32[]{:S(2)}, u32[]{:S(2)}) %collective-permute-start.4) | collective-permute-done | bytes 262176 | tf_op jit(solution)/shard_map/ppermute | solution.py:14
  69.1 4.5 %collective-permute-start.12 = (bf16[256,512]{1,0:T(8,128)(2,1)S(1)}, bf16[256,512]{1,0:T(8,128)(2,1)S(1)}, u32[]{:S(2)}, u32[]{:S(2)}) collective-permute-start(bf16[256,512]{1,0:T(8,128)(2,1)S(1)} %collective-permute-done.11), channel_id=1, source_target_pairs={{0,15},{1,0},{2,1},{3,2},{4,3},{5,4},{6,5},{7,6},{8,7},{9,8},{10,9... | collective-permute-start | bytes 786440 | tf_op jit(solution)/shard_map/ppermute | solution.py:16
  73.6 4.8 %collective-permute-done.5 = bf16[256,512]{1,0:T(8,128)(2,1)S(1)} collective-permute-done((bf16[256,512]{1,0:T(8,128)(2,1)S(1)}, bf16[256,512]{1,0:T(8,128)(2,1)S(1)}, u32[]{:S(2)}, u32[]{:S(2)}) %collective-permute-start.5) | collective-permute-done | bytes 262176 | tf_op jit(solution)/shard_map/ppermute | solution.py:14
  79.5 32.9 %all_gather.13 = bf16[2048,128]{1,0:T(8,128)(2,1)S(1)} all-gather(bf16[128,128]{1,0:T(8,128)(2,1)S(1)} %reshape.30), channel_id=1, replica_groups=mesh['groups'=2,'pts'=16] {'pts'}, dimensions={0}, use_global_device_ids=true | all-gather | bytes 557056 | tf_op jit(solution)/shard_map/all_gather | solution.py:37
  112.4 4.0 %reshape.31 = bf16[16384,16]{1,0:T(8,128)(2,1)} reshape(bf16[2048,128]{1,0:T(8,128)(2,1)S(1)} %all_gather.13) | data formatting | bytes 1048576 | tf_op jit(solution)/shard_map/reshape | solution.py:38
  116.4 4.3 %collective-permute-start.13 = (bf16[256,512]{1,0:T(8,128)(2,1)S(1)}, bf16[256,512]{1,0:T(8,128)(2,1)}, u32[]{:S(2)}, u32[]{:S(2)}) collective-permute-start(bf16[256,512]{1,0:T(8,128)(2,1)S(1)} %collective-permute-done.12), channel_id=1, source_target_pairs={{0,15},{1,0},{2,1},{3,2},{4,3},{5,4},{6,5},{7,6},{8,7},{9,8},{10,9... | collective-permute-start | bytes 786440 | tf_op jit(solution)/shard_map/ppermute | solution.py:16
  120.7 15.3 %convolution_convert_fusion = bf16[1024,16]{0,1:T(8,128)(2,1)S(1)} fusion(bf16[1024,16384]{1,0:T(8,128)(2,1)} %param.9, bf16[16384,16]{1,0:T(8,128)(2,1)} %reshape.31), kind=kOutput, calls=%fused_computation.12 | convolution fusion | flops 536887296 | bytes 34111488 | tf_op jit(solution)/shard_map/dot_general | solution.py:40
  136.3 23.3 %all_gather.14 = bf16[2048,128]{1,0:T(8,128)(2,1)S(1)} all-gather(bf16[128,128]{1,0:T(8,128)(2,1)S(1)} %reshape.32), channel_id=1, replica_groups=mesh['groups'=2,'pts'=16] {'pts'}, dimensions={0}, use_global_device_ids=true | all-gather | bytes 557056 | tf_op jit(solution)/shard_map/all_gather | solution.py:47
  159.6 4.1 %reshape.33 = bf16[16384,16]{1,0:T(8,128)(2,1)} reshape(bf16[2048,128]{1,0:T(8,128)(2,1)S(1)} %all_gather.14) | data formatting | bytes 1048576 | tf_op jit(solution)/shard_map/reshape | solution.py:50
  163.8 1.7 constant_dynamic-update-slice_fusion.31
  165.5 1.7 constant_dynamic-update-slice_fusion.30
  179.1 1.7 constant_dynamic-update-slice_fusion.15
  180.8 1.7 constant_dynamic-update-slice_fusion.14
  191.1 1.7 constant_dynamic-update-slice_fusion.1
  193.6 11.8 %subtract_convert_fusion = (bf16[256,16]{0,1:T(8,128)(2,1)S(1)}, f32[256,16]{0,1:T(8,128)}) fusion(s32[256]{0:T(256)S(1)} %copy-done.4, f32[16]{0:T(128)S(1)} %copy-done.5, bf16[16384,16]{1,0:T(8,128)(2,1)} %reshape.33, bf16[256,512]{1,0:T(8,128)(2,1)S(1)} %copy-done.1, bf16[16384,512]{1,0:T(8,128)(2,1)} %all-gather.2.cloned.1.call-done), kind=kOutput, calls=%fused_computation.46 | convolution fusion | flops 4450189312 | bytes 17589312 | tf_op jit(solution)/shard_map/dot_general | solution.py:51
  205.6 20.3 %all_gather.15 = bf16[512,128]{1,0:T(8,128)(2,1)S(1)} all-gather(bf16[32,128]{1,0:T(8,128)(2,1)S(1)} %reshape.34), channel_id=1, replica_groups=mesh['groups'=2,'pts'=16] {'pts'}, dimensions={0}, use_global_device_ids=true | all-gather | bytes 139264 | tf_op jit(solution)/shard_map/all_gather | solution.py:57
  226.6 12.9 %fusion.14 = bf16[1024,16]{1,0:T(8,128)(2,1)S(1)} fusion(bf16[4096,16]{1,0:T(8,128)(2,1)S(1)} %reshape.35, bf16[1024,512]{1,0:T(8,128)(2,1)S(1)} %copy-done, bf16[8192,512]{1,0:T(8,128)(2,1)} %constant_dynamic-update-slice_fusion, s32[]{:T(128)S(6)} %select_n.14), kind=kOutput, calls=%fused_computation.11 | convolution fusion | flops 4450189312 | bytes 5406724 | tf_op jit(solution)/shard_map/dot_general | solution.py:61
  239.5 13.1 %convolution_bitcast_fusion = f32[16384,16]{0,1:T(8,128)S(1)} fusion(bf16[1024,16]{1,0:T(8,128)(2,1)S(1)} %fusion.14, bf16[1024,16384]{1,0:T(8,128)(2,1)} %param.9), kind=kOutput, calls=%fused_computation.5 | convolution fusion | flops 536870912 | bytes 34635776 | tf_op jit(solution)/shard_map/dot_general | solution.py:69
  252.6 4.6 %copy.11 = f32[16384,16]{1,0:T(8,128)} copy(f32[16384,16]{0,1:T(8,128)S(1)} %convolution_bitcast_fusion) | data formatting | bytes 2097152 | tf_op jit(solution)/shard_map/dot_general | solution.py:69
  257.2 6.5 %reshape.36 = f32[2048,128]{1,0:T(8,128)} reshape(f32[16384,16]{1,0:T(8,128)} %copy.11) | data formatting | bytes 2097152 | tf_op jit(solution)/shard_map/reshape | solution.py:73
  263.7 55.2 %reduce-scatter.2.cloned.1.call-done = f32[128,128]{1,0:T(8,128)} async-done(((f32[2048,128]{1,0:T(8,128)}), f32[128,128]{1,0:T(8,128)}) %reduce-scatter.2.cloned.1.call-update) | async-done | bytes 65552 | tf_op jit(solution)/shard_map/reduce_scatter | solution.py:72
  (68 shorter events, 26.9 us)
Async XLA Ops:
  7.2 186.4 %all-gather.2.cloned.1.call-start = ((), (), s32[]{:S(2)}) async-start(), calls=%async_computation.1 | async-start | bytes 17825792 | tf_op jit(solution)/shard_map/all_gather | solution.py:46
  7.9 311.0 %reduce-scatter.2.cloned.1.call-start = ((), (), s32[]{:S(2)}) async-start(), calls=%async_computation.2 | async-start | bytes 1114112 | tf_op jit(solution)/shard_map/reduce_scatter | solution.py:72
  7.9 9.8 %collective-permute-start = (bf16[256,512]{1,0:T(8,128)(2,1)}, bf16[256,512]{1,0:T(8,128)(2,1)S(1)}, u32[]{:S(2)}, u32[]{:S(2)}) collective-permute-start(bf16[256,512]{1,0:T(8,128)(2,1)} %param.6), channel_id=1, source_target_pairs={{0,1},{1,2},{2,3},{3,4},{4,5},{5,6},{6,7},{7,8},{8,9},{9,10},{10,1... | collective-permute-start | bytes 786440 | tf_op jit(solution)/shard_map/ppermute | solution.py:14
  17.7 8.6 %collective-permute-start.1 = (bf16[256,512]{1,0:T(8,128)(2,1)S(1)}, bf16[256,512]{1,0:T(8,128)(2,1)S(1)}, u32[]{:S(2)}, u32[]{:S(2)}) collective-permute-start(bf16[256,512]{1,0:T(8,128)(2,1)S(1)} %collective-permute-done), channel_id=1, source_target_pairs={{0,1},{1,2},{2,3},{3,4},{4,5},{5,6},{6,7},{7,8},{8,9},{9,10},{10,1... | collective-permute-start | bytes 786440 | tf_op jit(solution)/shard_map/ppermute | solution.py:14
  17.7 14.2 %collective-permute-start.8 = (bf16[256,512]{1,0:T(8,128)(2,1)}, bf16[256,512]{1,0:T(8,128)(2,1)S(1)}, u32[]{:S(2)}, u32[]{:S(2)}) collective-permute-start(bf16[256,512]{1,0:T(8,128)(2,1)} %param.6), channel_id=1, source_target_pairs={{0,15},{1,0},{2,1},{3,2},{4,3},{5,4},{6,5},{7,6},{8,7},{9,8},{10,9... | collective-permute-start | bytes 786440 | tf_op jit(solution)/shard_map/ppermute | solution.py:16
  26.3 14.2 %collective-permute-start.2 = (bf16[256,512]{1,0:T(8,128)(2,1)S(1)}, bf16[256,512]{1,0:T(8,128)(2,1)S(1)}, u32[]{:S(2)}, u32[]{:S(2)}) collective-permute-start(bf16[256,512]{1,0:T(8,128)(2,1)S(1)} %collective-permute-done.1), channel_id=1, source_target_pairs={{0,1},{1,2},{2,3},{3,4},{4,5},{5,6},{6,7},{7,8},{8,9},{9,10},{10,1... | collective-permute-start | bytes 786440 | tf_op jit(solution)/shard_map/ppermute | solution.py:14
  32.0 14.2 %collective-permute-start.9 = (bf16[256,512]{1,0:T(8,128)(2,1)S(1)}, bf16[256,512]{1,0:T(8,128)(2,1)S(1)}, u32[]{:S(2)}, u32[]{:S(2)}) collective-permute-start(bf16[256,512]{1,0:T(8,128)(2,1)S(1)} %collective-permute-done.8), channel_id=1, source_target_pairs={{0,15},{1,0},{2,1},{3,2},{4,3},{5,4},{6,5},{7,6},{8,7},{9,8},{10,9... | collective-permute-start | bytes 786440 | tf_op jit(solution)/shard_map/ppermute | solution.py:16
  40.6 14.2 %collective-permute-start.3 = (bf16[256,512]{1,0:T(8,128)(2,1)S(1)}, bf16[256,512]{1,0:T(8,128)(2,1)S(1)}, u32[]{:S(2)}, u32[]{:S(2)}) collective-permute-start(bf16[256,512]{1,0:T(8,128)(2,1)S(1)} %collective-permute-done.2), channel_id=1, source_target_pairs={{0,1},{1,2},{2,3},{3,4},{4,5},{5,6},{6,7},{7,8},{8,9},{9,10},{10,1... | collective-permute-start | bytes 786440 | tf_op jit(solution)/shard_map/ppermute | solution.py:14
  46.1 14.2 %collective-permute-start.10 = (bf16[256,512]{1,0:T(8,128)(2,1)S(1)}, bf16[256,512]{1,0:T(8,128)(2,1)S(1)}, u32[]{:S(2)}, u32[]{:S(2)}) collective-permute-start(bf16[256,512]{1,0:T(8,128)(2,1)S(1)} %collective-permute-done.9), channel_id=1, source_target_pairs={{0,15},{1,0},{2,1},{3,2},{4,3},{5,4},{6,5},{7,6},{8,7},{9,8},{10,9... | collective-permute-start | bytes 786440 | tf_op jit(solution)/shard_map/ppermute | solution.py:16
  54.8 14.2 %collective-permute-start.4 = (bf16[256,512]{1,0:T(8,128)(2,1)S(1)}, bf16[256,512]{1,0:T(8,128)(2,1)S(1)}, u32[]{:S(2)}, u32[]{:S(2)}) collective-permute-start(bf16[256,512]{1,0:T(8,128)(2,1)S(1)} %collective-permute-done.3), channel_id=1, source_target_pairs={{0,1},{1,2},{2,3},{3,4},{4,5},{5,6},{6,7},{7,8},{8,9},{9,10},{10,1... | collective-permute-start | bytes 786440 | tf_op jit(solution)/shard_map/ppermute | solution.py:14
  60.4 8.7 %collective-permute-start.11 = (bf16[256,512]{1,0:T(8,128)(2,1)S(1)}, bf16[256,512]{1,0:T(8,128)(2,1)S(1)}, u32[]{:S(2)}, u32[]{:S(2)}) collective-permute-start(bf16[256,512]{1,0:T(8,128)(2,1)S(1)} %collective-permute-done.10), channel_id=1, source_target_pairs={{0,15},{1,0},{2,1},{3,2},{4,3},{5,4},{6,5},{7,6},{8,7},{9,8},{10,9... | collective-permute-start | bytes 786440 | tf_op jit(solution)/shard_map/ppermute | solution.py:16
  69.1 9.3 %collective-permute-start.5 = (bf16[256,512]{1,0:T(8,128)(2,1)S(1)}, bf16[256,512]{1,0:T(8,128)(2,1)S(1)}, u32[]{:S(2)}, u32[]{:S(2)}) collective-permute-start(bf16[256,512]{1,0:T(8,128)(2,1)S(1)} %collective-permute-done.4), channel_id=1, source_target_pairs={{0,1},{1,2},{2,3},{3,4},{4,5},{5,6},{6,7},{7,8},{8,9},{9,10},{10,1... | collective-permute-start | bytes 786440 | tf_op jit(solution)/shard_map/ppermute | solution.py:14
  69.1 47.3 %collective-permute-start.12 = (bf16[256,512]{1,0:T(8,128)(2,1)S(1)}, bf16[256,512]{1,0:T(8,128)(2,1)S(1)}, u32[]{:S(2)}, u32[]{:S(2)}) collective-permute-start(bf16[256,512]{1,0:T(8,128)(2,1)S(1)} %collective-permute-done.11), channel_id=1, source_target_pairs={{0,15},{1,0},{2,1},{3,2},{4,3},{5,4},{6,5},{7,6},{8,7},{9,8},{10,9... | collective-permute-start | bytes 786440 | tf_op jit(solution)/shard_map/ppermute | solution.py:16
  78.4 42.3 %copy-start.2 = (bf16[256,512]{1,0:T(8,128)(2,1)}, bf16[256,512]{1,0:T(8,128)(2,1)S(1)}, u32[]{:S(2)}) copy-start(bf16[256,512]{1,0:T(8,128)(2,1)S(1)} %collective-permute-done.5) | copy-start | bytes 786436
  78.4 42.3 %collective-permute-start.6 = (bf16[256,512]{1,0:T(8,128)(2,1)S(1)}, bf16[256,512]{1,0:T(8,128)(2,1)}, u32[]{:S(2)}, u32[]{:S(2)}) collective-permute-start(bf16[256,512]{1,0:T(8,128)(2,1)S(1)} %collective-permute-done.5), channel_id=1, source_target_pairs={{0,1},{1,2},{2,3},{3,4},{4,5},{5,6},{6,7},{7,8},{8,9},{9,10},{10,1... | collective-permute-start | bytes 786440 | tf_op jit(solution)/shard_map/ppermute | solution.py:14
  116.4 47.3 %collective-permute-start.13 = (bf16[256,512]{1,0:T(8,128)(2,1)S(1)}, bf16[256,512]{1,0:T(8,128)(2,1)}, u32[]{:S(2)}, u32[]{:S(2)}) collective-permute-start(bf16[256,512]{1,0:T(8,128)(2,1)S(1)} %collective-permute-done.12), channel_id=1, source_target_pairs={{0,15},{1,0},{2,1},{3,2},{4,3},{5,4},{6,5},{7,6},{8,7},{9,8},{10,9... | collective-permute-start | bytes 786440 | tf_op jit(solution)/shard_map/ppermute | solution.py:16
  120.7 43.1 %collective-permute-start.7 = (bf16[256,512]{1,0:T(8,128)(2,1)}, bf16[256,512]{1,0:T(8,128)(2,1)}, u32[]{:S(2)}, u32[]{:S(2)}) collective-permute-start(bf16[256,512]{1,0:T(8,128)(2,1)} %collective-permute-done.6), channel_id=1, source_target_pairs={{0,1},{1,2},{2,3},{3,4},{4,5},{5,6},{6,7},{7,8},{8,9},{9,10},{10,1... | collective-permute-start | bytes 786440 | tf_op jit(solution)/shard_map/ppermute | solution.py:14
  135.9 36.5 %copy-start.1 = (bf16[256,512]{1,0:T(8,128)(2,1)S(1)}, bf16[256,512]{1,0:T(8,128)(2,1)}, u32[]{:S(2)}) copy-start(bf16[256,512]{1,0:T(8,128)(2,1)} %param.6) | copy-start | bytes 786436
  163.7 18.8 %copy-start.3 = (bf16[256,512]{1,0:T(8,128)(2,1)S(1)}, bf16[256,512]{1,0:T(8,128)(2,1)}, u32[]{:S(2)}) copy-start(bf16[256,512]{1,0:T(8,128)(2,1)} %copy-done.2) | copy-start | bytes 786436
  163.7 29.9 %copy-start.4 = (s32[256]{0:T(256)S(1)}, s32[256]{0:T(256)}, u32[]{:S(2)}) copy-start(s32[256]{0:T(256)} %param.7) | copy-start | bytes 3076
  163.7 29.9 %copy-start.5 = (f32[16]{0:T(128)S(1)}, f32[16]{0:T(128)}, u32[]{:S(2)}) copy-start(f32[16]{0:T(128)} %param.11) | copy-start | bytes 196
  163.7 14.7 %collective-permute-start.14 = (bf16[256,512]{1,0:T(8,128)(2,1)}, bf16[256,512]{1,0:T(8,128)(2,1)S(1)}, u32[]{:S(2)}, u32[]{:S(2)}) collective-permute-start(bf16[256,512]{1,0:T(8,128)(2,1)} %collective-permute-done.13), channel_id=1, source_target_pairs={{0,15},{1,0},{2,1},{3,2},{4,3},{5,4},{6,5},{7,6},{8,7},{9,8},{10,9... | collective-permute-start | bytes 786440 | tf_op jit(solution)/shard_map/ppermute | solution.py:16
  193.5 33.0 %copy-start = (bf16[1024,512]{1,0:T(8,128)(2,1)S(1)}, bf16[1024,512]{1,0:T(8,128)(2,1)}, u32[]{:S(2)}) copy-start(bf16[1024,512]{1,0:T(8,128)(2,1)} %param.8) | copy-start | bytes 3145732
Sparse Core Ops, SparseCore 0:
  10.1 154.9 all-gather.1
  263.8 55.0 reduce-scatter.1
